TPU v7x, 32 devices: a whole 2x2x4 slice. The times are simulated.
32 devices in a mesh: rows: 4 (over x, core), cols: 8 (over z, y).
Axes of the slice: x: 2, y: 2, z: 4, core: 2. Of those that a mesh axis runs over, the one named last changes fastest.
Arguments:
- pair_integrals: float32 [4096, 4096], P('rows', 'cols'), may hold values from -6 to 6
- left_factor: float32 [4096, 1024], P('rows', 'cols'), may hold values from -0.9375 to 0.9375
- core: float32 [1024, 1024], replicated, may hold values from -6 to 6
- right_factor: float32 [4096, 1024], P('cols', 'rows'), may hold values from -0.9375 to 0.9375
Outputs:
- core_next: float32 [1024, 1024], replicated
All inputs are finite; a program needn't handle non-finite values.
Results may differ from a plain program's by a relative error of at most 0.000062.
Values sent between devices are 32-bit elements; how exact they have to be, the bound alone decides.
No kernel may reach another device: no remote copies, remote signals or barrier semaphores. Data moves between devices by JAX's collectives and lax.ppermute only.
A program may use at most 128 MiB of HBM per device.

v0:
```python
import jax
import jax.numpy as jnp
from jax import lax
from jax.sharding import PartitionSpec as P


def product(left, right):
    return jnp.dot(left, right, precision=lax.Precision.HIGHEST, preferred_element_type=jnp.float32)


def shards(pair_integrals, left_factor, core, right_factor):
    left_rows = lax.all_gather(left_factor, "cols", axis=1, tiled=True)
    right_rows = lax.all_gather(right_factor, "rows", axis=1, tiled=True)
    mixed = product(core, right_rows.T)
    residual = pair_integrals - product(left_rows, mixed)
    along = product(residual, right_rows)
    local_term = product(left_rows.T, along)
    gradient = lax.psum(local_term, ("rows", "cols"))
    numer = jnp.sum(gradient * gradient)
    image = product(left_rows, product(gradient, right_rows.T))
    denom = lax.psum(jnp.sum(image * image), ("rows", "cols"))
    return core + numer / denom * gradient


def solution(mesh):
    return jax.shard_map(
        shards,
        mesh=mesh,
        in_specs=(P("rows", "cols"), P("rows", "cols"), P(), P("cols", "rows")),
        out_specs=P(),
        check_vma=False,
    )
```

profile of v0, /device:TPU:0, one launch (start us, length us, event | category | flops | bytes accessed | tf_op | source)
XLA Modules:
  0.0 382.5 jit_solution(6131846957028007544)
XLA Ops:
  6.5 0.0 all-gather.3.cloned.1.call-start
  6.5 0.7 all-gather.3.cloned.1.call-update
  7.3 0.0 all-gather.5.cloned.1.call-start
  7.3 0.7 all-gather.5.cloned.1.call-update
  8.0 0.0 all-reduce.2.cloned.1.call-start
  8.1 26.2 %all-gather.3.cloned.1.call-done = f32[512,1024]{1,0:T(8,128)} async-done(((f32[512,256]{1,0:T(8,128)}), f32[512,1024]{1,0:T(8,128)}) %all-gather.3.cloned.1.call-update) | async-done | bytes 2097168 | tf_op jit(solution)/shard_map/all_gather | solution.py:13
  34.2 10.2 %fusion.1 = f32[1024,512]{1,0:T(8,128)} fusion(f32[1024,1024]{1,0:T(8,128)} %param.6, f32[512,1024]{1,0:T(8,128)} %all-gather.3.cloned.1.call-done), kind=kOutput, calls=%fused_computation.6 | convolution fusion | flops 6442450944 | bytes 8388608 | tf_op jit(solution)/shard_map/dot_general | solution.py:8
  44.5 0.0 copy-start
  44.5 66.5 %all-gather.5.cloned.1.call-done = f32[1024,1024]{1,0:T(8,128)} async-done(((f32[1024,128]{1,0:T(8,128)}), f32[1024,1024]{1,0:T(8,128)}) %all-gather.5.cloned.1.call-update) | async-done | bytes 4194320 | tf_op jit(solution)/shard_map/all_gather | solution.py:12
  110.9 0.0 copy-start.3
  110.9 9.6 %fusion.2 = f32[512,1024]{0,1:T(8,128)S(1)} fusion(f32[1024,512]{1,0:T(8,128)} %fusion.1, f32[1024,1024]{1,0:T(8,128)} %all-gather.5.cloned.1.call-done), kind=kOutput, calls=%fused_computation.7 | convolution fusion | flops 6442450944 | bytes 8388608 | tf_op jit(solution)/shard_map/dot_general | solution.py:8
  120.6 0.0 copy-done
  120.6 0.0 copy-done.3
  120.6 0.0 copy-start.1
  120.6 6.9 %fusion = f32[1024,1024]{1,0:T(8,128)S(1)} fusion(f32[512,1024]{1,0:T(8,128)S(1)} %copy-done, f32[1024,512]{1,0:T(8,128)S(1)} %copy-done.3, f32[512,1024]{0,1:T(8,128)S(1)} %fusion.2), kind=kOutput, calls=%fused_computation.4 | convolution fusion | flops 6442975232 | bytes 10485760 | tf_op jit(solution)/shard_map/dot_general | solution.py:8
  127.5 0.0 copy-done.1
  127.5 15.0 %convolution_bitcast_fusion = f32[1024,1024]{0,1:T(8,128)} fusion(f32[1024,1024]{1,0:T(8,128)S(1)} %fusion, f32[1024,1024]{1,0:T(8,128)S(1)} %copy-done.1), kind=kOutput, calls=%fused_computation.2 | convolution fusion | flops 12884901888 | bytes 12582912 | tf_op jit(solution)/shard_map/dot_general | solution.py:8
  142.5 0.0 all-reduce.2.cloned.1.call-update
  142.5 140.8 %all-reduce.2.cloned.1.call-done = f32[1024,1024]{0,1:T(8,128)} async-done(((f32[1024,1024]{0,1:T(8,128)}), f32[1024,1024]{0,1:T(8,128)}) %all-reduce.2.cloned.1.call-update) | async-done | bytes 4194320 | tf_op jit(solution)/shard_map/psum | solution.py:18
  283.3 0.0 copy-start.2
  283.3 15.9 %fusion.3 = f32[1024,512]{1,0:T(8,128)S(1)} fusion(f32[1024,1024]{0,1:T(8,128)} %all-reduce.2.cloned.1.call-done, f32[512,1024]{1,0:T(8,128)S(1)} %copy-done), kind=kOutput, calls=%fused_computation.8 | convolution fusion | flops 6442450944 | bytes 8388608 | tf_op jit(solution)/shard_map/dot_general | solution.py:8
  299.2 0.0 copy-done.2
  299.2 14.3 %multiply_reduce_fusion.1 = f32[]{:T(128)} fusion(f32[1024,512]{1,0:T(8,128)S(1)} %fusion.3, f32[1024,1024]{1,0:T(8,128)S(1)} %copy-done.2), kind=kOutput, calls=%fused_computation.5 | convolution fusion | flops 6443499520 | bytes 6291460 | tf_op jit(solution)/shard_map/dot_general | solution.py:8
  313.5 5.3 %copy.5 = f32[1024,1024]{0,1:T(8,128)} copy(f32[1024,1024]{1,0:T(8,128)} %param.6) | data formatting | bytes 8388608 | tf_op args[2]
  318.8 39.5 %psum.15 = f32[]{:T(128)} all-reduce(f32[]{:T(128)} %multiply_reduce_fusion.1), channel_id=1, replica_groups=mesh['rows'=4,'cols'=8] {'rows','cols'}, use_global_device_ids=true, to_apply=%region_3.0 | all-reduce | flops 1 | bytes 8 | tf_op jit(solution)/shard_map/psum | solution.py:21
  358.3 3.9 %multiply_reduce_fusion = f32[]{:T(128)} fusion(f32[1024,1024]{0,1:T(8,128)} %all-reduce.2.cloned.1.call-done), kind=kLoop, calls=%fused_computation.1 | loop fusion | flops 2097151 | bytes 4194308 | tf_op jit(solution)/shard_map/reduce_sum | solution.py:19
  363.6 6.9 %multiply_add_fusion = f32[1024,1024]{0,1:T(8,128)} fusion(f32[1024,1024]{0,1:T(8,128)} %copy.5, f32[1024,1024]{0,1:T(8,128)} %all-reduce.2.cloned.1.call-done, f32[]{:T(128)S(6)} %div.3), kind=kLoop, calls=%fused_computation | loop fusion | flops 2097152 | bytes 12582916 | tf_op jit(solution)/shard_map/add | solution.py:22
  370.4 5.3 %copy.6 = f32[1024,1024]{1,0:T(8,128)} copy(f32[1024,1024]{0,1:T(8,128)} %multiply_add_fusion) | data formatting | bytes 8388608 | tf_op jit(solution)/shard_map/add | solution.py:22
Async XLA Ops:
  6.5 27.7 %all-gather.3.cloned.1.call-start = ((), (), s32[]{:S(2)}) async-start(), calls=%async_computation | async-start | bytes 2621440 | tf_op jit(solution)/shard_map/all_gather | solution.py:13
  7.3 103.7 %all-gather.5.cloned.1.call-start = ((), (), s32[]{:S(2)}) async-start(), calls=%async_computation.1 | async-start | bytes 4718592 | tf_op jit(solution)/shard_map/all_gather | solution.py:12
  8.0 275.3 %all-reduce.2.cloned.1.call-start = ((), (), s32[]{:S(2)}) async-start(), calls=%async_computation.2 | async-start | bytes 8388608 | tf_op jit(solution)/shard_map/psum | solution.py:18
  44.5 76.1 %copy-start = (f32[512,1024]{1,0:T(8,128)S(1)}, f32[512,1024]{1,0:T(8,128)}, u32[]{:S(2)}) copy-start(f32[512,1024]{1,0:T(8,128)} %all-gather.3.cloned.1.call-done) | copy-start | bytes 6291460
  110.9 9.7 %copy-start.3 = (f32[1024,512]{1,0:T(8,128)S(1)}, f32[1024,512]{1,0:T(8,128)}, u32[]{:S(2)}) copy-start(f32[1024,512]{1,0:T(8,128)} %param.4) | copy-start | bytes 6291460
  120.6 6.9 %copy-start.1 = (f32[1024,1024]{1,0:T(8,128)S(1)}, f32[1024,1024]{1,0:T(8,128)}, u32[]{:S(2)}) copy-start(f32[1024,1024]{1,0:T(8,128)} %all-gather.5.cloned.1.call-done) | copy-start | bytes 12582916
  283.3 15.9 %copy-start.2 = (f32[1024,1024]{1,0:T(8,128)S(1)}, f32[1024,1024]{1,0:T(8,128)}, u32[]{:S(2)}) copy-start(f32[1024,1024]{1,0:T(8,128)} %all-gather.5.cloned.1.call-done) | copy-start | bytes 12582916
Sparse Core Ops, SparseCore 0:
  8.9 25.2 all-gather.2
  36.2 74.6 all-gather.4
  142.6 140.6 all-reduce.1
where the time goes:
time: 389 us; the launch traced here: 383 us
  waiting for transfers between devices  235 us (60%)
  matrix products  71.9 us (18%)
  blocking collectives  39.5 us (10%)
  between operations  14.7 us (4%)
  other arithmetic  10.8 us (3%)
  local copies, waits for them, and re-layouts  10.7 us (3%)
    psum x1, waiting for transfers between devices, shards(): gradient = lax.psum(local_term, ('rows', 'cols'))  141 us
    dot_general x6, matrix products, product(): jnp.dot(left, right, precision=lax.Precision.HIGHEST, preferred_element_t...  71.9 us
    all_gather x1, waiting for transfers between devices, shards(): left_rows = lax.all_gather(left_factor, 'cols', axis=1, tiled=True)  66.5 us
    psum x1, blocking collectives, shards(): denom = lax.psum(jnp.sum(image * image), ('rows', 'cols'))  39.5 us
    all_gather x1, waiting for transfers between devices, shards(): right_rows = lax.all_gather(right_factor, 'rows', axis=1, tiled=True)  26.2 us
  transfers between devices with their start and end apart: 3, of which 3 were waited for; matrix products, arithmetic and copies ran while one was open for 3% of the time, Pallas kernels for 0%

commit v1 on v0

v1 whole, which is shorter than its diff:
```python
import jax
import jax.numpy as jnp
from jax import lax
from jax.sharding import PartitionSpec as P


def dot(left, right, contract):
    return lax.dot_general(
        left,
        right,
        (contract, ((), ())),
        precision=lax.Precision.HIGH,
        preferred_element_type=jnp.float32,
    )


def pick(array, index, axis):
    return lax.dynamic_index_in_dim(array, index, axis, keepdims=False)


def solution(mesh):
    rows, cols = mesh.shape["rows"], mesh.shape["cols"]
    nx, nz = rows // 2, cols // 2

    def swap_core(a):
        return lax.ppermute(a, "rows", [(i, i ^ 1) for i in range(rows)])

    def shift_x(a, d):
        return lax.ppermute(a, "rows", [(i, (i + 2 * d) % rows) for i in range(rows)])

    def swap_y(a):
        return lax.ppermute(a, "cols", [(i, i ^ 1) for i in range(cols)])

    def shift_z(a, d):
        return lax.ppermute(a, "cols", [(i, (i + 2 * d) % cols) for i in range(cols)])

    def shards(pair_integrals, left_factor, core, right_factor):
        row, col = lax.axis_index("rows"), lax.axis_index("cols")
        x, c, z, y = row // 2, row % 2, col // 2, col % 2
        rank = core.shape[0]
        height, block = left_factor.shape
        width, part = right_factor.shape
        sub = block // rows

        left_t = jnp.zeros((nz, 2, block, height), jnp.float32)
        held = left_factor.T
        for d in range(nz):
            if d > 0:
                held = shift_z(held, 1)
            other = swap_y(held)
            at = (z - d) % nz
            left_t = lax.dynamic_update_slice(left_t, held[None, None], (at, y, 0, 0))
            left_t = lax.dynamic_update_slice(left_t, other[None, None], (at, 1 - y, 0, 0))
        left_t = left_t.reshape(rank, height)

        blocks = {}
        for d in range(nx):
            mine = right_factor if d == 0 else shift_x(right_factor, d)
            blocks[d, 0], blocks[d, 1] = mine, swap_core(mine)
        ordered = []
        for i in range(nx):
            for j in range(2):
                one = blocks[0, 0]
                for d in range(nx):
                    for e in range(2):
                        hit = ((x - d) % nx == i) & (c ^ e == j)
                        one = jnp.where(hit, blocks[d, e], one)
                ordered.append(one)
        right = jnp.concatenate(ordered, axis=1)

        mixed = dot(core, right, ((1,), (1,)))
        residual = pair_integrals - dot(left_t, mixed, ((0,), (0,)))
        across = dot(left_t, residual, ((1,), (0,))).reshape(nz, 2, nx, 2, sub, width)

        across = pick(across, c, 3) + swap_core(pick(across, 1 - c, 3))
        total = pick(across, x, 2)
        for d in range(1, nx):
            total = total + shift_x(pick(across, (x + d) % nx, 2), d)

        term = dot(total.reshape(nz * 2 * sub, width), right, ((1,), (0,)))
        term = term.reshape(nz, 2, sub, rank)
        term = pick(term, y, 1) + swap_y(pick(term, 1 - y, 1))
        own = pick(term, z, 0)
        for d in range(1, nz):
            own = own + shift_z(pick(term, (z + d) % nz, 0), d)
        numer = jnp.sum(own * own)

        line = jnp.zeros((nz, sub, rank), jnp.float32)
        for d in range(nz):
            piece = own if d == 0 else shift_z(own, d)
            line = lax.dynamic_update_slice(line, piece[None], ((z - d) % nz, 0, 0))
        half = nz // 2
        first, second = line[:half], line[half:]
        first = {0: first, 1: swap_y(first)}
        second = {(0, d): second if d == 0 else shift_x(second, d) for d in range(nx)}
        pieces = []
        joined = jnp.concatenate([first[0], first[1]])
        for d in range(nx):
            got = joined if d == 0 else shift_x(joined, d)
            pieces.append((0, 0, d, got[:half]))
            pieces.append((0, 1, d, got[half:]))
        joined = jnp.concatenate([second[0, d] for d in range(nx)])
        got = swap_y(joined)
        for d in range(nx):
            pieces.append((half, 0, d, second[0, d]))
            pieces.append((half, 1, d, got[d * half:(d + 1) * half]))
        gradient = jnp.zeros((nz, 2, nx, 2, sub, rank), jnp.float32)
        for start, e, d, value in pieces:
            for f in range(2):
                value = value if f == 0 else swap_core(value)
                gradient = lax.dynamic_update_slice(
                    gradient,
                    value[:, None, None, None],
                    (start, y ^ e, (x - d) % nx, c ^ f, 0, 0),
                )
        gradient = gradient.reshape(rank, rank)

        inner = dot(gradient, right, ((1,), (1,)))
        image = dot(left_t, inner, ((0,), (0,)))
        sums = jnp.stack([numer, jnp.sum(image * image)]).reshape(1, 2)
        sums = sums + swap_core(sums)
        sums = sum((shift_x(sums, d) for d in range(1, nx)), sums)
        sums = sums + swap_y(sums)
        step = 1
        while step < nz:
            sums = sums + shift_z(sums, step)
            step *= 2
        return core + sums[0, 0] / sums[0, 1] * gradient

    return jax.shard_map(
        shards,
        mesh=mesh,
        in_specs=(P("rows", "cols"), P("rows", "cols"), P(), P("cols", "rows")),
        out_specs=P(),
        check_vma=False,
    )
```

time: 389 us -> 198 us (0.51); the launches traced: 383 us -> 198 us
  waiting for transfers between devices: 235 us -> 103 us
  matrix products: 71.9 us -> 26 us
  blocking collectives: 39.5 us -> 0 us
  starting transfers between devices: 0.08 us -> 32.9 us
  local copies, waits for them, and re-layouts: 10.7 us -> 24.5 us
  between operations: 14.7 us -> 1.84 us
    psum x1 -> x0, waiting for transfers between devices: 141 us -> none  [shards(): gradient = lax.psum(local_term, ('rows', 'cols'))]
    ppermute x0 -> x36, waiting for transfers between devices: none -> 103 us  [the longest x11 52.1 us: shift_z(): lax.ppermute(a, 'cols', [(i, (i + 2 * d) % cols) for i in range(cols)])]
    all_gather x2 -> x0, waiting for transfers between devices: 92.6 us -> none  [the longest x1 66.5 us: shards(): left_rows = lax.all_gather(left_factor, 'cols', axis=1, tiled=True)]
    dot_general x6, matrix products: 71.9 us -> 26 us  [dot(): lax.dot_general(left, right, (contract, ((), ())), precision=lax.Precisio...]
    psum x1 -> x0, blocking collectives: 39.5 us -> none  [shards(): denom = lax.psum(jnp.sum(image * image), ('rows', 'cols'))]
    ppermute x0 -> x36, starting transfers between devices: none -> 32.9 us  [the longest x11 14 us: shift_z(): lax.ppermute(a, 'cols', [(i, (i + 2 * d) % cols) for i in range(cols)])]
    dynamic_update_slice x0 -> x29, local copies, waits for them, and re-layouts: none -> 16.7 us  [the longest x5 11.8 us: shards(): left_t = lax.dynamic_update_slice(left_t, held[None, None], (at, y, 0, 0))]
    add x1 -> x0, local copies, waits for them, and re-layouts: 5.34 us -> none  [shards(): return core + numer / denom * gradient]
  transfers between devices with their start and end apart: 3 -> 36, of which waited for: 3 -> 23; matrix products, arithmetic and copies ran while one was open for 3% -> 11% of each run, Pallas kernels for 0% -> 0%
where the time goes in v1:
time: 198 us
  waiting for transfers between devices  103 us (52%)
  starting transfers between devices  32.9 us (17%)
  matrix products  26 us (13%)
  local copies, waits for them, and re-layouts  24.5 us (12%)
  other arithmetic  9.57 us (5%)
    ppermute x11, waiting for transfers between devices, shift_z(): lax.ppermute(a, 'cols', [(i, (i + 2 * d) % cols) for i in range(cols)])  52.1 us
    dot_general x6, matrix products, dot(): lax.dot_general(left, right, (contract, ((), ())), precision=lax.Precisio...  26 us
    ppermute x5, waiting for transfers between devices, shift_x(): lax.ppermute(a, 'rows', [(i, (i + 2 * d) % rows) for i in range(rows)])  25.9 us
    ppermute x8, waiting for transfers between devices, swap_y(): return lax.ppermute(a, 'cols', [(i, i ^ 1) for i in range(cols)])  19.2 us
    ppermute x11, starting transfers between devices, shift_z(): lax.ppermute(a, 'cols', [(i, (i + 2 * d) % cols) for i in range(cols)])  14 us
    dynamic_update_slice x5, local copies, waits for them, and re-layouts, shards(): left_t = lax.dynamic_update_slice(left_t, held[None, None], (at, y, 0, 0))  11.8 us
    ppermute x8, starting transfers between devices, swap_y(): return lax.ppermute(a, 'cols', [(i, i ^ 1) for i in range(cols)])  8.92 us
    ppermute x5, starting transfers between devices, shift_x(): lax.ppermute(a, 'rows', [(i, (i + 2 * d) % rows) for i in range(rows)])  7.59 us
  transfers between devices with their start and end apart: 36, of which 23 were waited for; matrix products, arithmetic and copies ran while one was open for 11% of the time, Pallas kernels for 0%

profile of v1, /device:TPU:0, one launch (start us, length us, event | category | flops | bytes accessed | tf_op | source)
XLA Modules:
  0.0 197.9 jit_solution(5665885486374958583)
XLA Ops:
  0.0 3.1 %collective-permute-start.1 = (f32[128,1024]{0,1:T(8,128)}, f32[128,1024]{0,1:T(8,128)}, u32[]{:S(2)}, u32[]{:S(2)}) collective-permute-start(f32[128,1024]{0,1:T(8,128)} %bitcast.147), channel_id=1, source_target_pairs={{0,2},{1,3},{2,4},{3,5},{4,6},{5,7},{6,0},{7,1},{8,10},{9,11},{10,... | collective-permute-start | bytes 1572872 | tf_op jit(solution)/shard_map/ppermute | solution.py:35
  3.1 1.5 collective-permute-start.7
  4.5 1.5 collective-permute-start
  6.1 11.3 %collective-permute-done.1 = f32[128,1024]{0,1:T(8,128)} collective-permute-done((f32[128,1024]{0,1:T(8,128)}, f32[128,1024]{0,1:T(8,128)}, u32[]{:S(2)}, u32[]{:S(2)}) %collective-permute-start.1) | collective-permute-done | bytes 524320 | tf_op jit(solution)/shard_map/ppermute | solution.py:35
  17.4 2.4 %broadcast_in_dim.93 = f32[4,2,128,1024]{2,3,1,0:T(8,128)} broadcast(f32[]{:T(128)} %constant.190.clone.1), dimensions={} | broadcast | bytes 4194308 | tf_op jit(solution)/shard_map/broadcast_in_dim | solution.py:45
  19.8 0.8 bitcast_dynamic-update-slice_fusion
  20.6 1.5 collective-permute-start.2
  22.1 0.8 bitcast_dynamic-update-slice_fusion.6
  22.9 1.9 bitcast_dynamic-update-slice_fusion.5
  24.8 7.8 %collective-permute-done.3 = f32[128,1024]{0,1:T(8,128)} collective-permute-done((f32[128,1024]{0,1:T(8,128)}, f32[128,1024]{0,1:T(8,128)}, u32[]{:S(2)}, u32[]{:S(2)}) %collective-permute-start.3) | collective-permute-done | bytes 524320 | tf_op jit(solution)/shard_map/ppermute | solution.py:35
  32.6 1.4 collective-permute-start.4
  34.3 3.5 %fusion.7 = f32[512,1024]{1,0:T(8,128)S(1)} fusion(f32[1024,1024]{1,0:T(8,128)S(1)} %copy-done.2, f32[512,256]{1,0:T(8,128)S(1)} %get-tuple-element.8, f32[512,256]{1,0:T(8,128)S(1)} %get-tuple-element.9, f32[512,256]{1,0:T(8,128)S(1)} %get-tuple-element.10, f32[512,256]{1,0:T(8,128)S(1)} %get-tuple-element.7), kind=kOutput, calls=%fused_computation.29 | convolution fusion | flops 3222798336 | bytes 8388608 | tf_op jit(solution)/shard_map/dot_general | solution.py:8
  37.8 0.8 bitcast_dynamic-update-slice_fusion.4
  38.6 9.2 %collective-permute-done.5 = f32[128,1024]{0,1:T(8,128)} collective-permute-done((f32[128,1024]{0,1:T(8,128)}, f32[128,1024]{0,1:T(8,128)}, u32[]{:S(2)}, u32[]{:S(2)}) %collective-permute-start.5) | collective-permute-done | bytes 524320 | tf_op jit(solution)/shard_map/ppermute | solution.py:35
  47.9 0.8 collective-permute-start.6
  48.7 1.9 bitcast_dynamic-update-slice_fusion.3
  50.6 0.8 bitcast_dynamic-update-slice_fusion.2
  51.4 1.9 bitcast_dynamic-update-slice_fusion.1
  53.3 5.4 %copy.5 = f32[4,2,128,1024]{3,2,1,0:T(8,128)} copy(f32[4,2,128,1024]{2,3,1,0:T(8,128)} %bitcast_dynamic-update-slice_fusion.1) | data formatting | bytes 8388608 | tf_op jit(solution)/shard_map/dynamic_update_slice | solution.py:52
  59.1 2.0 %copy.6 = f32[1,1,128,1024]{3,2,1,0:T(8,128)} copy(f32[1,1,128,1024]{2,3,1,0:T(8,128)} %bitcast.8) | data formatting | bytes 1048576 | tf_op jit(solution)/shard_map/broadcast_in_dim | solution.py:53
  61.2 1.9 constant_dynamic-update-slice_fusion
  63.1 8.7 %fusion.19 = f32[1024,512]{1,0:T(8,128)S(1)} fusion(f32[1024,1024]{1,0:T(8,128)} %bitcast.144, f32[512,1024]{1,0:T(8,128)S(1)} %fusion.7), kind=kOutput, calls=%fused_computation.67 | convolution fusion | flops 3221225472 | bytes 8388608 | tf_op jit(solution)/shard_map/dot_general | solution.py:8
  71.8 3.4 %fusion.2 = f32[4,2,2,2,32,512]{5,4,3,2,1,0:T(8,128)S(1)} fusion(f32[4,2,2,2,32,1024]{5,4,3,2,1,0:T(8,128)S(1)} %bitcast.145, f32[1024,512]{1,0:T(8,128)S(1)} %copy-done.9, f32[1024,512]{1,0:T(8,128)S(1)} %fusion.19), kind=kOutput, calls=%fused_computation.4 | convolution fusion | flops 3221749760 | bytes 10485760 | tf_op jit(solution)/shard_map/dot_general | solution.py:8
  75.3 1.1 dynamic-slice_bitcast_fusion
  76.3 3.0 %collective-permute-done.10 = f32[4,2,2,32,512]{4,3,2,1,0:T(8,128)} collective-permute-done((f32[4,2,2,32,512]{4,3,2,1,0:T(8,128)}, f32[4,2,2,32,512]{4,3,2,1,0:T(8,128)}, u32[]{:S(2)}, u32[]{:S(2)}) %collective-permute-start.10) | collective-permute-done | bytes 1048608 | tf_op jit(solution)/shard_map/ppermute | solution.py:26
  79.3 1.4 bitcast_add_fusion
  80.8 1.0 copy-done.8
  81.8 1.6 collective-permute-start.11
  83.3 12.5 %collective-permute-done.11 = f32[4,2,32,512]{3,2,1,0:T(8,128)S(1)} collective-permute-done((f32[4,2,32,512]{3,2,1,0:T(8,128)S(1)}, f32[4,2,32,512]{3,2,1,0:T(8,128)S(1)}, u32[]{:S(2)}, u32[]{:S(2)}) %collective-permute-start.11) | collective-permute-done | bytes 524320 | tf_op jit(solution)/shard_map/ppermute | solution.py:29
  95.8 2.4 %fusion = f32[4,2,32,1024]{3,2,1,0:T(8,128)S(1)} fusion(f32[4,2,32,512]{3,2,1,0:T(8,128)S(1)} %collective-permute-done.11, f32[4,2,2,32,512]{4,3,2,1,0:T(8,128)} %copy-done.8, s32[]{:T(128)S(6)} %select_n.368, f32[512,256]{1,0:T(8,128)S(1)} %get-tuple-element.8, f32[512,256]{1,0:T(8,128)} %copy-done.4, f32[512,256]{1,0:T(8,128)} %copy-done.6, ...), kind=kOutput, calls=%fused_computation.2 | convolution fusion | flops 807010304 | bytes 4194308 | tf_op jit(solution)/shard_map/dot_general | solution.py:8
  98.3 1.0 collective-permute-start.12
  99.4 12.1 %collective-permute-done.12 = f32[4,32,1024]{2,1,0:T(8,128)S(1)} collective-permute-done((f32[4,32,1024]{2,1,0:T(8,128)S(1)}, f32[4,32,1024]{2,1,0:T(8,128)S(1)}, u32[]{:S(2)}, u32[]{:S(2)}) %collective-permute-start.12) | collective-permute-done | bytes 524320 | tf_op jit(solution)/shard_map/ppermute | solution.py:32
  111.6 2.5 %collective-permute-start.15 = (f32[32,1024]{1,0:T(8,128)S(1)}, f32[32,1024]{1,0:T(8,128)S(1)}, u32[]{:S(2)}, u32[]{:S(2)}) collective-permute-start(f32[32,1024]{1,0:T(8,128)S(1)} %get-tuple-element.18), channel_id=1, source_target_pairs={{0,6},{1,7},{2,0},{3,1},{4,2},{5,3},{6,4},{7,5},{8,14},{9,15},{10,... | collective-permute-start | bytes 393224 | tf_op jit(solution)/shard_map/ppermute | solution.py:35
  114.1 0.6 collective-permute-start.13
  114.7 3.2 %collective-permute-done.15 = f32[32,1024]{1,0:T(8,128)S(1)} collective-permute-done((f32[32,1024]{1,0:T(8,128)S(1)}, f32[32,1024]{1,0:T(8,128)S(1)}, u32[]{:S(2)}, u32[]{:S(2)}) %collective-permute-start.15) | collective-permute-done | bytes 131104 | tf_op jit(solution)/shard_map/ppermute | solution.py:35
  118.0 6.3 %collective-permute-done.14 = f32[32,1024]{1,0:T(8,128)S(1)} collective-permute-done((f32[32,1024]{1,0:T(8,128)S(1)}, f32[32,1024]{1,0:T(8,128)S(1)}, u32[]{:S(2)}, u32[]{:S(2)}) %collective-permute-start.14) | collective-permute-done | bytes 131104 | tf_op jit(solution)/shard_map/ppermute | solution.py:35
  124.3 0.6 multiply_reduce_fusion.1
  125.2 1.9 collective-permute-start.17
  127.1 2.9 %collective-permute-start.18 = (f32[32,1024]{1,0:T(8,128)S(1)}, f32[32,1024]{1,0:T(8,128)S(1)}, u32[]{:S(2)}, u32[]{:S(2)}) collective-permute-start(f32[32,1024]{1,0:T(8,128)S(1)} %get-tuple-element.6), channel_id=1, source_target_pairs={{0,6},{1,7},{2,0},{3,1},{4,2},{5,3},{6,4},{7,5},{8,14},{9,15},{10,... | collective-permute-start | bytes 393224 | tf_op jit(solution)/shard_map/ppermute | solution.py:35
  130.1 3.0 %collective-permute-done.16 = f32[32,1024]{1,0:T(8,128)S(1)} collective-permute-done((f32[32,1024]{1,0:T(8,128)S(1)}, f32[32,1024]{1,0:T(8,128)S(1)}, u32[]{:S(2)}, u32[]{:S(2)}) %collective-permute-start.16) | collective-permute-done | bytes 131104 | tf_op jit(solution)/shard_map/ppermute | solution.py:35
  133.1 3.8 %collective-permute-done.17 = f32[32,1024]{1,0:T(8,128)S(1)} collective-permute-done((f32[32,1024]{1,0:T(8,128)S(1)}, f32[32,1024]{1,0:T(8,128)S(1)}, u32[]{:S(2)}, u32[]{:S(2)}) %collective-permute-start.17) | collective-permute-done | bytes 131104 | tf_op jit(solution)/shard_map/ppermute | solution.py:35
  137.1 1.6 collective-permute-start.20
  139.2 1.5 collective-permute-start.26
  141.2 2.3 %collective-permute-done.20 = f32[2,32,1024]{2,1,0:T(8,128)S(1)} collective-permute-done((f32[2,32,1024]{2,1,0:T(8,128)S(1)}, f32[2,32,1024]{2,1,0:T(8,128)S(1)}, u32[]{:S(2)}, u32[]{:S(2)}) %collective-permute-start.20) | collective-permute-done | bytes 262176 | tf_op jit(solution)/shard_map/ppermute | solution.py:32
  143.5 1.6 collective-permute-start.22
  145.1 3.2 %collective-permute-done.26 = f32[2,32,1024]{2,1,0:T(8,128)S(1)} collective-permute-done((f32[2,32,1024]{2,1,0:T(8,128)S(1)}, f32[2,32,1024]{2,1,0:T(8,128)S(1)}, u32[]{:S(2)}, u32[]{:S(2)}) %collective-permute-start.26) | collective-permute-done | bytes 262176 | tf_op jit(solution)/shard_map/ppermute | solution.py:29
  149.5 1.0 collective-permute-done.21
  150.5 8.1 %collective-permute-done.22 = f32[4,32,1024]{2,1,0:T(8,128)S(1)} collective-permute-done((f32[4,32,1024]{2,1,0:T(8,128)S(1)}, f32[4,32,1024]{2,1,0:T(8,128)S(1)}, u32[]{:S(2)}, u32[]{:S(2)}) %collective-permute-start.22) | collective-permute-done | bytes 524320 | tf_op jit(solution)/shard_map/ppermute | solution.py:29
  159.2 1.2 collective-permute-done.27
  161.4 0.7 collective-permute-done.28
  162.5 3.5 %fusion.6 = f32[1024,512]{1,0:T(8,128)S(1)} fusion(f32[1024,1024]{1,0:T(8,128)S(1)} %bitcast.143, f32[512,256]{1,0:T(8,128)S(1)} %get-tuple-element.8, f32[512,256]{1,0:T(8,128)S(1)} %copy-done.5, f32[512,256]{1,0:T(8,128)S(1)} %copy-done.7, f32[512,256]{1,0:T(8,128)S(1)} %get-tuple-element.7), kind=kOutput, calls=%fused_computation.28 | convolution fusion | flops 3222798336 | bytes 8388608 | tf_op jit(solution)/shard_map/dot_general | solution.py:8
  166.1 4.4 %multiply_reduce_fusion = f32[]{:T(128)} fusion(f32[1024,1024]{1,0:T(8,128)S(1)} %bitcast.146, f32[1024,512]{1,0:T(8,128)S(1)} %fusion.6), kind=kOutput, calls=%fused_computation.6 | convolution fusion | flops 3222274048 | bytes 6291460 | tf_op jit(solution)/shard_map/dot_general | solution.py:8
  170.5 1.4 maximum_bitcast_fusion
  172.1 0.9 collective-permute-done.31
  173.0 1.4 fusion.27
  174.4 1.5 collective-permute-start.32
  175.9 2.1 %collective-permute-done.32 = f32[1,2]{1,0:T(1,128)S(1)} collective-permute-done((f32[1,2]{1,0:T(1,128)S(1)}, f32[1,2]{1,0:T(1,128)S(1)}, u32[]{:S(2)}, u32[]{:S(2)}) %collective-permute-start.32) | collective-permute-done | bytes 40 | tf_op jit(solution)/shard_map/ppermute | solution.py:29
  177.9 1.4 fusion.28
  179.8 3.1 %collective-permute-done.33 = f32[1,2]{1,0:T(1,128)S(1)} collective-permute-done((f32[1,2]{1,0:T(1,128)S(1)}, f32[1,2]{1,0:T(1,128)S(1)}, u32[]{:S(2)}, u32[]{:S(2)}) %collective-permute-start.33) | collective-permute-done | bytes 40 | tf_op jit(solution)/shard_map/ppermute | solution.py:32
  182.9 2.4 %collective-permute-start.34 = (f32[1,2]{1,0:T(1,128)S(1)}, f32[1,2]{1,0:T(1,128)S(1)}, u32[]{:S(2)}, u32[]{:S(2)}) collective-permute-start(f32[1,2]{1,0:T(1,128)S(1)} %add.287), channel_id=1, source_target_pairs={{0,2},{1,3},{2,4},{3,5},{4,6},{5,7},{6,0},{7,1},{8,10},{9,11},{10,... | collective-permute-start | bytes 32 | tf_op jit(solution)/shard_map/ppermute | solution.py:35
  185.3 3.2 %collective-permute-done.34 = f32[1,2]{1,0:T(1,128)S(1)} collective-permute-done((f32[1,2]{1,0:T(1,128)S(1)}, f32[1,2]{1,0:T(1,128)S(1)}, u32[]{:S(2)}, u32[]{:S(2)}) %collective-permute-start.34) | collective-permute-done | bytes 40 | tf_op jit(solution)/shard_map/ppermute | solution.py:35
  188.8 4.2 %collective-permute-done.35 = f32[1,2]{1,0:T(1,128)S(1)} collective-permute-done((f32[1,2]{1,0:T(1,128)S(1)}, f32[1,2]{1,0:T(1,128)S(1)}, u32[]{:S(2)}, u32[]{:S(2)}) %collective-permute-start.35) | collective-permute-done | bytes 40 | tf_op jit(solution)/shard_map/ppermute | solution.py:35
  192.9 0.6 fusion.18
  194.9 3.0 %multiply_add_fusion = f32[1024,1024]{1,0:T(8,128)} fusion(f32[1024,1024]{1,0:T(8,128)S(1)} %copy-done.3, f32[]{:T(128)} %bitcast.64, f32[4,2,2,2,32,1024]{5,4,3,2,1,0:T(8,128)S(1)} %bitcast_dynamic-update-slice_fusion.22), kind=kLoop, calls=%fused_computation | loop fusion | flops 2097152 | bytes 12582916 | tf_op jit(solution)/shard_map/add | solution.py:128
  (92 shorter events, 6.6 us)
Async XLA Ops:
  0.0 19.8 %copy-start.11 = (f32[1024,128]{1,0:T(8,128)S(1)}, f32[1024,128]{1,0:T(8,128)}, u32[]{:S(2)}) copy-start(f32[1024,128]{1,0:T(8,128)} %param.5) | copy-start | bytes 1572868
  0.0 34.0 %copy-start.10 = (f32[512,256]{1,0:T(8,128)S(1)}, f32[512,256]{1,0:T(8,128)}, u32[]{:S(2)}) copy-start(f32[512,256]{1,0:T(8,128)} %param.7) | copy-start | bytes 1572868
  0.0 17.4 %collective-permute-start.1 = (f32[128,1024]{0,1:T(8,128)}, f32[128,1024]{0,1:T(8,128)}, u32[]{:S(2)}, u32[]{:S(2)}) collective-permute-start(f32[128,1024]{0,1:T(8,128)} %bitcast.147), channel_id=1, source_target_pairs={{0,2},{1,3},{2,4},{3,5},{4,6},{5,7},{6,0},{7,1},{8,10},{9,11},{10,... | collective-permute-start | bytes 1572872 | tf_op jit(solution)/shard_map/ppermute | solution.py:35
  3.1 14.3 %collective-permute-start.7 = (f32[512,256]{1,0:T(8,128)}, f32[512,256]{1,0:T(8,128)S(1)}, u32[]{:S(2)}, u32[]{:S(2)}) collective-permute-start(f32[512,256]{1,0:T(8,128)} %param.7), channel_id=1, source_target_pairs={{0,16},{8,24},{16,0},{24,8},{1,17},{9,25},{17,1},{25,9},{2,18},{10... | collective-permute-start | bytes 1572872 | tf_op jit(solution)/shard_map/ppermute | solution.py:29
  4.5 17.6 %collective-permute-start = (f32[128,1024]{0,1:T(8,128)}, f32[128,1024]{0,1:T(8,128)S(1)}, u32[]{:S(2)}, u32[]{:S(2)}) collective-permute-start(f32[128,1024]{0,1:T(8,128)} %bitcast.148), channel_id=1, source_target_pairs={{0,1},{1,0},{2,3},{3,2},{4,5},{5,4},{6,7},{7,6},{8,9},{9,8},{10,11... | collective-permute-start | bytes 1572872 | tf_op jit(solution)/shard_map/ppermute | solution.py:32
  6.1 27.9 %collective-permute-start.9 = (f32[512,256]{1,0:T(8,128)}, f32[512,256]{1,0:T(8,128)S(1)}, u32[]{:S(2)}, u32[]{:S(2)}) collective-permute-start(f32[512,256]{1,0:T(8,128)} %param.7), channel_id=1, source_target_pairs={{0,8},{8,0},{16,24},{24,16},{1,9},{9,1},{17,25},{25,17},{2,10},{10... | collective-permute-start | bytes 1572872 | tf_op jit(solution)/shard_map/ppermute | solution.py:26
  17.4 15.2 %collective-permute-start.3 = (f32[128,1024]{0,1:T(8,128)}, f32[128,1024]{0,1:T(8,128)}, u32[]{:S(2)}, u32[]{:S(2)}) collective-permute-start(f32[128,1024]{0,1:T(8,128)} %collective-permute-done.1), channel_id=1, source_target_pairs={{0,2},{1,3},{2,4},{3,5},{4,6},{5,7},{6,0},{7,1},{8,10},{9,11},{10,... | collective-permute-start | bytes 1572872 | tf_op jit(solution)/shard_map/ppermute | solution.py:35
  17.4 16.6 %collective-permute-start.8 = (f32[512,256]{1,0:T(8,128)S(1)}, f32[512,256]{1,0:T(8,128)S(1)}, u32[]{:S(2)}, u32[]{:S(2)}) collective-permute-start(f32[512,256]{1,0:T(8,128)S(1)} %collective-permute-done.7), channel_id=1, source_target_pairs={{0,8},{8,0},{16,24},{24,16},{1,9},{9,1},{17,25},{25,17},{2,10},{10... | collective-permute-start | bytes 1572872 | tf_op jit(solution)/shard_map/ppermute | solution.py:26
  20.6 13.7 %copy-start.2 = (f32[1024,1024]{1,0:T(8,128)S(1)}, f32[1024,1024]{1,0:T(8,128)}, u32[]{:S(2)}) copy-start(f32[1024,1024]{1,0:T(8,128)} %param.6) | copy-start | bytes 12582916
  20.6 17.2 %collective-permute-start.2 = (f32[128,1024]{0,1:T(8,128)}, f32[128,1024]{0,1:T(8,128)S(1)}, u32[]{:S(2)}, u32[]{:S(2)}) collective-permute-start(f32[128,1024]{0,1:T(8,128)} %collective-permute-done.1), channel_id=1, source_target_pairs={{0,1},{1,0},{2,3},{3,2},{4,5},{5,4},{6,7},{7,6},{8,9},{9,8},{10,11... | collective-permute-start | bytes 1572872 | tf_op jit(solution)/shard_map/ppermute | solution.py:32
  32.6 18.0 %collective-permute-start.4 = (f32[128,1024]{0,1:T(8,128)}, f32[128,1024]{0,1:T(8,128)S(1)}, u32[]{:S(2)}, u32[]{:S(2)}) collective-permute-start(f32[128,1024]{0,1:T(8,128)} %collective-permute-done.3), channel_id=1, source_target_pairs={{0,1},{1,0},{2,3},{3,2},{4,5},{5,4},{6,7},{7,6},{8,9},{9,8},{10,11... | collective-permute-start | bytes 1572872 | tf_op jit(solution)/shard_map/ppermute | solution.py:32
  34.0 13.9 %collective-permute-start.5 = (f32[128,1024]{0,1:T(8,128)}, f32[128,1024]{0,1:T(8,128)}, u32[]{:S(2)}, u32[]{:S(2)}) collective-permute-start(f32[128,1024]{0,1:T(8,128)} %collective-permute-done.3), channel_id=1, source_target_pairs={{0,2},{1,3},{2,4},{3,5},{4,6},{5,7},{6,0},{7,1},{8,10},{9,11},{10,... | collective-permute-start | bytes 1572872 | tf_op jit(solution)/shard_map/ppermute | solution.py:35
  34.2 3.6 %copy-start.4 = (f32[512,256]{1,0:T(8,128)}, f32[512,256]{1,0:T(8,128)S(1)}, u32[]{:S(2)}) copy-start(f32[512,256]{1,0:T(8,128)S(1)} %get-tuple-element.9) | copy-start | bytes 1572868
  34.2 3.6 %copy-start.6 = (f32[512,256]{1,0:T(8,128)}, f32[512,256]{1,0:T(8,128)S(1)}, u32[]{:S(2)}) copy-start(f32[512,256]{1,0:T(8,128)S(1)} %get-tuple-element.10) | copy-start | bytes 1572868
  47.9 11.3 %collective-permute-start.6 = (f32[128,1024]{0,1:T(8,128)}, f32[128,1024]{0,1:T(8,128)}, u32[]{:S(2)}, u32[]{:S(2)}) collective-permute-start(f32[128,1024]{0,1:T(8,128)} %collective-permute-done.5), channel_id=1, source_target_pairs={{0,1},{1,0},{2,3},{3,2},{4,5},{5,4},{6,7},{7,6},{8,9},{9,8},{10,11... | collective-permute-start | bytes 1572872 | tf_op jit(solution)/shard_map/ppermute | solution.py:32
  63.0 8.7 %copy-start = (f32[4,2,128,1024]{3,2,1,0:T(8,128)S(1)}, f32[4,2,128,1024]{3,2,1,0:T(8,128)}, u32[]{:S(2)}) copy-start(f32[4,2,128,1024]{3,2,1,0:T(8,128)} %constant_dynamic-update-slice_fusion) | copy-start | bytes 12582916
  63.1 8.7 %copy-start.9 = (f32[1024,512]{1,0:T(8,128)S(1)}, f32[1024,512]{1,0:T(8,128)}, u32[]{:S(2)}) copy-start(f32[1024,512]{1,0:T(8,128)} %param.4) | copy-start | bytes 6291460
  76.3 3.0 %collective-permute-start.10 = (f32[4,2,2,32,512]{4,3,2,1,0:T(8,128)}, f32[4,2,2,32,512]{4,3,2,1,0:T(8,128)}, u32[]{:S(2)}, u32[]{:S(2)}) collective-permute-start(f32[4,2,2,32,512]{4,3,2,1,0:T(8,128)} %dynamic-slice_bitcast_fusion), channel_id=1, source_target_pairs={{0,8},{8,0},{16,24},{24,16},{1,9},{9,1},{17,25},{25,17},{2,10},{10... | collective-permute-start | bytes 3145736 | tf_op jit(solution)/shard_map/ppermute | solution.py:26
  80.8 1.0 copy-start.8
  81.8 14.0 %collective-permute-start.11 = (f32[4,2,32,512]{3,2,1,0:T(8,128)S(1)}, f32[4,2,32,512]{3,2,1,0:T(8,128)S(1)}, u32[]{:S(2)}, u32[]{:S(2)}) collective-permute-start(f32[4,2,32,512]{3,2,1,0:T(8,128)S(1)} %dynamic-slice_bitcast_fusion.2), channel_id=1, source_target_pairs={{0,16},{8,24},{16,0},{24,8},{1,17},{9,25},{17,1},{25,9},{2,18},{10... | collective-permute-start | bytes 1572872 | tf_op jit(solution)/shard_map/ppermute | solution.py:29
  98.3 13.2 %collective-permute-start.12 = (f32[4,32,1024]{2,1,0:T(8,128)S(1)}, f32[4,32,1024]{2,1,0:T(8,128)S(1)}, u32[]{:S(2)}, u32[]{:S(2)}) collective-permute-start(f32[4,32,1024]{2,1,0:T(8,128)S(1)} %dynamic-slice_bitcast_fusion.1), channel_id=1, source_target_pairs={{0,1},{1,0},{2,3},{3,2},{4,5},{5,4},{6,7},{7,6},{8,9},{9,8},{10,11... | collective-permute-start | bytes 1572872 | tf_op jit(solution)/shard_map/ppermute | solution.py:32
  111.6 6.4 %collective-permute-start.15 = (f32[32,1024]{1,0:T(8,128)S(1)}, f32[32,1024]{1,0:T(8,128)S(1)}, u32[]{:S(2)}, u32[]{:S(2)}) collective-permute-start(f32[32,1024]{1,0:T(8,128)S(1)} %get-tuple-element.18), channel_id=1, source_target_pairs={{0,6},{1,7},{2,0},{3,1},{4,2},{5,3},{6,4},{7,5},{8,14},{9,15},{10,... | collective-permute-start | bytes 393224 | tf_op jit(solution)/shard_map/ppermute | solution.py:35
  114.1 10.2 %collective-permute-start.14 = (f32[32,1024]{1,0:T(8,128)S(1)}, f32[32,1024]{1,0:T(8,128)S(1)}, u32[]{:S(2)}, u32[]{:S(2)}) collective-permute-start(f32[32,1024]{1,0:T(8,128)S(1)} %get-tuple-element.19), channel_id=1, source_target_pairs={{0,4},{1,5},{2,6},{3,7},{4,0},{5,1},{6,2},{7,3},{8,12},{9,13},{10,... | collective-permute-start | bytes 393224 | tf_op jit(solution)/shard_map/ppermute | solution.py:35
  114.1 10.2 %collective-permute-start.13 = (f32[32,1024]{1,0:T(8,128)S(1)}, f32[32,1024]{1,0:T(8,128)S(1)}, u32[]{:S(2)}, u32[]{:S(2)}) collective-permute-start(f32[32,1024]{1,0:T(8,128)S(1)} %get-tuple-element.17), channel_id=1, source_target_pairs={{0,2},{1,3},{2,4},{3,5},{4,6},{5,7},{6,0},{7,1},{8,10},{9,11},{10,... | collective-permute-start | bytes 393224 | tf_op jit(solution)/shard_map/ppermute | solution.py:35
  124.9 8.2 %collective-permute-start.16 = (f32[32,1024]{1,0:T(8,128)S(1)}, f32[32,1024]{1,0:T(8,128)S(1)}, u32[]{:S(2)}, u32[]{:S(2)}) collective-permute-start(f32[32,1024]{1,0:T(8,128)S(1)} %get-tuple-element.6), channel_id=1, source_target_pairs={{0,2},{1,3},{2,4},{3,5},{4,6},{5,7},{6,0},{7,1},{8,10},{9,11},{10,... | collective-permute-start | bytes 393224 | tf_op jit(solution)/shard_map/ppermute | solution.py:35
  125.2 11.8 %collective-permute-start.17 = (f32[32,1024]{1,0:T(8,128)S(1)}, f32[32,1024]{1,0:T(8,128)S(1)}, u32[]{:S(2)}, u32[]{:S(2)}) collective-permute-start(f32[32,1024]{1,0:T(8,128)S(1)} %get-tuple-element.6), channel_id=1, source_target_pairs={{0,4},{1,5},{2,6},{3,7},{4,0},{5,1},{6,2},{7,3},{8,12},{9,13},{10,... | collective-permute-start | bytes 393224 | tf_op jit(solution)/shard_map/ppermute | solution.py:35
  127.1 9.9 %collective-permute-start.18 = (f32[32,1024]{1,0:T(8,128)S(1)}, f32[32,1024]{1,0:T(8,128)S(1)}, u32[]{:S(2)}, u32[]{:S(2)}) collective-permute-start(f32[32,1024]{1,0:T(8,128)S(1)} %get-tuple-element.6), channel_id=1, source_target_pairs={{0,6},{1,7},{2,0},{3,1},{4,2},{5,3},{6,4},{7,5},{8,14},{9,15},{10,... | collective-permute-start | bytes 393224 | tf_op jit(solution)/shard_map/ppermute | solution.py:35
  137.1 6.4 %collective-permute-start.20 = (f32[2,32,1024]{2,1,0:T(8,128)S(1)}, f32[2,32,1024]{2,1,0:T(8,128)S(1)}, u32[]{:S(2)}, u32[]{:S(2)}) collective-permute-start(f32[2,32,1024]{2,1,0:T(8,128)S(1)} %get-tuple-element.14), channel_id=1, source_target_pairs={{0,1},{1,0},{2,3},{3,2},{4,5},{5,4},{6,7},{7,6},{8,9},{9,8},{10,11... | collective-permute-start | bytes 786440 | tf_op jit(solution)/shard_map/ppermute | solution.py:32
  138.7 10.3 %collective-permute-start.19 = (f32[2,32,1024]{2,1,0:T(8,128)S(1)}, f32[2,32,1024]{2,1,0:T(8,128)S(1)}, u32[]{:S(2)}, u32[]{:S(2)}) collective-permute-start(f32[2,32,1024]{2,1,0:T(8,128)S(1)} %get-tuple-element.14), channel_id=1, source_target_pairs={{0,8},{8,0},{16,24},{24,16},{1,9},{9,1},{17,25},{25,17},{2,10},{10... | collective-permute-start | bytes 786440 | tf_op jit(solution)/shard_map/ppermute | solution.py:26
  138.7 22.7 %collective-permute-start.25 = (f32[2,32,1024]{2,1,0:T(8,128)S(1)}, f32[2,32,1024]{2,1,0:T(8,128)S(1)}, u32[]{:S(2)}, u32[]{:S(2)}) collective-permute-start(f32[2,32,1024]{2,1,0:T(8,128)S(1)} %get-tuple-element.13), channel_id=1, source_target_pairs={{0,8},{8,0},{16,24},{24,16},{1,9},{9,1},{17,25},{25,17},{2,10},{10... | collective-permute-start | bytes 786440 | tf_op jit(solution)/shard_map/ppermute | solution.py:26
  139.2 9.2 %collective-permute-start.26 = (f32[2,32,1024]{2,1,0:T(8,128)S(1)}, f32[2,32,1024]{2,1,0:T(8,128)S(1)}, u32[]{:S(2)}, u32[]{:S(2)}) collective-permute-start(f32[2,32,1024]{2,1,0:T(8,128)S(1)} %get-tuple-element.13), channel_id=1, source_target_pairs={{0,16},{8,24},{16,0},{24,8},{1,17},{9,25},{17,1},{25,9},{2,18},{10... | collective-permute-start | bytes 786440 | tf_op jit(solution)/shard_map/ppermute | solution.py:29
  143.5 15.1 %collective-permute-start.22 = (f32[4,32,1024]{2,1,0:T(8,128)S(1)}, f32[4,32,1024]{2,1,0:T(8,128)S(1)}, u32[]{:S(2)}, u32[]{:S(2)}) collective-permute-start(f32[4,32,1024]{2,1,0:T(8,128)S(1)} %pad_maximum_fusion.1), channel_id=1, source_target_pairs={{0,16},{8,24},{16,0},{24,8},{1,17},{9,25},{17,1},{25,9},{2,18},{10... | collective-permute-start | bytes 1572872 | tf_op jit(solution)/shard_map/ppermute | solution.py:29
  148.4 12.1 %collective-permute-start.27 = (f32[4,32,1024]{2,1,0:T(8,128)S(1)}, f32[4,32,1024]{2,1,0:T(8,128)S(1)}, u32[]{:S(2)}, u32[]{:S(2)}) collective-permute-start(f32[4,32,1024]{2,1,0:T(8,128)S(1)} %pad_maximum_fusion.2), channel_id=1, source_target_pairs={{0,1},{1,0},{2,3},{3,2},{4,5},{5,4},{6,7},{7,6},{8,9},{9,8},{10,11... | collective-permute-start | bytes 1572872 | tf_op jit(solution)/shard_map/ppermute | solution.py:32
  149.0 1.5 collective-permute-start.21
  149.0 13.2 %collective-permute-start.29 = (f32[2,32,1024]{2,1,0:T(8,128)S(1)}, f32[2,32,1024]{2,1,0:T(8,128)S(1)}, u32[]{:S(2)}, u32[]{:S(2)}) collective-permute-start(f32[2,32,1024]{2,1,0:T(8,128)S(1)} %collective-permute-done.26), channel_id=1, source_target_pairs={{0,8},{8,0},{16,24},{24,16},{1,9},{9,1},{17,25},{25,17},{2,10},{10... | collective-permute-start | bytes 786440 | tf_op jit(solution)/shard_map/ppermute | solution.py:26
  150.5 12.0 %copy-start.5 = (f32[512,256]{1,0:T(8,128)S(1)}, f32[512,256]{1,0:T(8,128)}, u32[]{:S(2)}) copy-start(f32[512,256]{1,0:T(8,128)} %copy-done.4) | copy-start | bytes 1572868
  150.5 12.0 %copy-start.7 = (f32[512,256]{1,0:T(8,128)S(1)}, f32[512,256]{1,0:T(8,128)}, u32[]{:S(2)}) copy-start(f32[512,256]{1,0:T(8,128)} %copy-done.6) | copy-start | bytes 1572868
  158.7 2.0 collective-permute-start.23
  158.7 2.5 %collective-permute-start.24 = (f32[2,32,1024]{2,1,0:T(8,128)S(1)}, f32[2,32,1024]{2,1,0:T(8,128)S(1)}, u32[]{:S(2)}, u32[]{:S(2)}) collective-permute-start(f32[2,32,1024]{2,1,0:T(8,128)S(1)} %get-tuple-element.15), channel_id=1, source_target_pairs={{0,8},{8,0},{16,24},{24,16},{1,9},{9,1},{17,25},{25,17},{2,10},{10... | collective-permute-start | bytes 786440 | tf_op jit(solution)/shard_map/ppermute | solution.py:26
  160.5 1.6 collective-permute-start.28
  160.6 1.9 collective-permute-start.30
  162.5 3.5 %copy-start.1 = (f32[4,2,128,1024]{3,2,1,0:T(8,128)S(1)}, f32[4,2,128,1024]{3,2,1,0:T(8,128)}, u32[]{:S(2)}) copy-start(f32[4,2,128,1024]{3,2,1,0:T(8,128)} %constant_dynamic-update-slice_fusion) | copy-start | bytes 12582916
  166.0 28.8 %copy-start.3 = (f32[1024,1024]{1,0:T(8,128)S(1)}, f32[1024,1024]{1,0:T(8,128)}, u32[]{:S(2)}) copy-start(f32[1024,1024]{1,0:T(8,128)} %param.6) | copy-start | bytes 12582916
  171.8 1.2 collective-permute-start.31
  174.4 3.6 %collective-permute-start.32 = (f32[1,2]{1,0:T(1,128)S(1)}, f32[1,2]{1,0:T(1,128)S(1)}, u32[]{:S(2)}, u32[]{:S(2)}) collective-permute-start(f32[1,2]{1,0:T(1,128)S(1)} %fusion.27), channel_id=1, source_target_pairs={{0,16},{8,24},{16,0},{24,8},{1,17},{9,25},{17,1},{25,9},{2,18},{10... | collective-permute-start | bytes 32 | tf_op jit(solution)/shard_map/ppermute | solution.py:29
  179.3 3.6 %collective-permute-start.33 = (f32[1,2]{1,0:T(1,128)S(1)}, f32[1,2]{1,0:T(1,128)S(1)}, u32[]{:S(2)}, u32[]{:S(2)}) collective-permute-start(f32[1,2]{1,0:T(1,128)S(1)} %fusion.28), channel_id=1, source_target_pairs={{0,1},{1,0},{2,3},{3,2},{4,5},{5,4},{6,7},{7,6},{8,9},{9,8},{10,11... | collective-permute-start | bytes 32 | tf_op jit(solution)/shard_map/ppermute | solution.py:32
  182.9 5.6 %collective-permute-start.34 = (f32[1,2]{1,0:T(1,128)S(1)}, f32[1,2]{1,0:T(1,128)S(1)}, u32[]{:S(2)}, u32[]{:S(2)}) collective-permute-start(f32[1,2]{1,0:T(1,128)S(1)} %add.287), channel_id=1, source_target_pairs={{0,2},{1,3},{2,4},{3,5},{4,6},{5,7},{6,0},{7,1},{8,10},{9,11},{10,... | collective-permute-start | bytes 32 | tf_op jit(solution)/shard_map/ppermute | solution.py:35
  188.5 4.5 %collective-permute-start.35 = (f32[1,2]{1,0:T(1,128)S(1)}, f32[1,2]{1,0:T(1,128)S(1)}, u32[]{:S(2)}, u32[]{:S(2)}) collective-permute-start(f32[1,2]{1,0:T(1,128)S(1)} %add.288), channel_id=1, source_target_pairs={{0,4},{1,5},{2,6},{3,7},{4,0},{5,1},{6,2},{7,3},{8,12},{9,13},{10,... | collective-permute-start | bytes 32 | tf_op jit(solution)/shard_map/ppermute | solution.py:35
